TPU v7x, 32 devices: a whole 2x2x4 slice. The times are simulated.
32 devices in a mesh: batch: 8 (over z, y), wide: 4 (over x, core).
Axes of the slice: x: 2, y: 2, z: 4, core: 2. Of those that a mesh axis runs over, the one named last changes fastest.
Arguments:
- tokens: bfloat16 [16384, 768], P(('batch', 'wide')), may hold values from -6 to 6
- block_row: int32 [128], P(('batch', 'wide')), may hold values from 0 to 3, as said below
- block_live: int32 [128], P(('batch', 'wide')), may hold values from 0 to 128, as said below
- query_weight: float32 [768, 768], P(('batch', 'wide')), may hold values from -0.21875 to 0.21875
- key_weight: float32 [768, 768], P(('batch', 'wide')), may hold values from -0.21875 to 0.21875
- value_weight: float32 [768, 768], P(('batch', 'wide')), may hold values from -0.21875 to 0.21875
- out_weight: float32 [768, 768], P(('batch', 'wide')), may hold values from -2.5 to 2.5
- position_bias: float32 [12, 1024], replicated, may hold values from -3 to 3
- features: float32 [64, 64], replicated, may hold values from -5 to 5
- up_weight: float32 [768, 3072], P('batch', 'wide'), may hold values from -0.21875 to 0.21875
- up_bias: float32 [3072], replicated, may hold values from -1.5 to 1.5
- down_weight: float32 [768, 3072], P('batch', 'wide'), may hold values from -0.109375 to 0.109375
- down_bias: float32 [768], replicated, may hold values from -1.5 to 1.5
- gain_one: float32 [768], replicated, may hold values from 0.5 to 1.5
- shift_one: float32 [768], replicated, may hold values from -1 to 1
- gain_two: float32 [768], replicated, may hold values from 0.5 to 1.5
- shift_two: float32 [768], replicated, may hold values from -1 to 1
- cotangent: bfloat16 [16384, 768], P(('batch', 'wide')), may hold values from -6 to 6
Outputs:
- out_tokens: bfloat16 [16384, 768], P(('batch', 'wide'))
- grad_tokens: float32 [16384, 768], P(('batch', 'wide'))
- grad_query_weight: float32 [768, 768], P(('batch', 'wide'))
- grad_key_weight: float32 [768, 768], P(('batch', 'wide'))
- grad_value_weight: float32 [768, 768], P(('batch', 'wide'))
- grad_out_weight: float32 [768, 768], P(('batch', 'wide'))
- grad_position_bias: float32 [12, 1024], replicated
- grad_up_weight: float32 [768, 3072], P('batch', 'wide')
- grad_up_bias: float32 [3072], replicated
- grad_down_weight: float32 [768, 3072], P('batch', 'wide')
- grad_down_bias: float32 [768], replicated
- grad_gain_one: float32 [768], replicated
- grad_shift_one: float32 [768], replicated
- grad_gain_two: float32 [768], replicated
- grad_shift_two: float32 [768], replicated
Inputs may be any that keep to these rules, and one draw needn't show every extreme that they name: `block_row`: in each device's 512 // 128 entries the row numbers start at 0 and rise by one at the first block of each row; a row covers an aligned run of a power of two blocks, from one block to all of a device's blocks. `block_live`: the live tokens of a row are its first ones and more than half of its blocks' slots; a one-block row is full.
All inputs are finite; a program needn't handle non-finite values.
Results may differ from a plain program's by a relative error of at most 0.018.
Values may be sent and summed in bfloat16 or wider, within the bound.
No kernel may reach another device: no remote copies, remote signals or barrier semaphores. Data moves between devices by JAX's collectives and lax.ppermute only.
A program may use at most 192 MiB of HBM per device.

v0:
```python
from functools import partial
import jax
import jax.numpy as jnp
from jax import lax
from jax.sharding import PartitionSpec as P

BLK = 128
eps = 1e-05
highest = lax.Precision.HIGHEST
rows_contract = (((0,), (0,)), ((), ()))
cols_contract = (((1,), (1,)), ((), ()))


def token_masks(block_row, block_live, width):
    blocks = block_row.shape[0]
    offsets = jnp.broadcast_to(jnp.arange(width, dtype=jnp.int32)[None, :], (blocks, width))
    row_ids = jnp.broadcast_to(block_row[:, None], (blocks, width)).reshape(-1)
    live_tok = (offsets < block_live[:, None]).astype(jnp.float32).reshape(-1)
    return (row_ids, live_tok)


def toeplitz_from(vector, length):
    flipped = vector[::-1]
    tiled_flat = jnp.broadcast_to(flipped[None, :], (length, 2 * length)).reshape(-1)
    return tiled_flat[: length * (2 * length - 1)].reshape(length, 2 * length - 1)[:, length - 1 :]


def diagonal_sums(matrix, length):
    padded = jnp.concatenate([jnp.zeros((length, length), jnp.float32), matrix], axis=1).reshape(-1)
    padded = jnp.concatenate([padded, jnp.zeros((length,), jnp.float32)])
    column_sums = jnp.sum(padded.reshape(length, 2 * length + 1), axis=0)
    return column_sums[::-1][: 2 * length]


def feature_map(head_part, features):
    scaled = head_part * head_part.shape[-1] ** (-0.25)
    projected = jnp.einsum("thd,df->thf", scaled, features, precision=highest)
    return jnp.exp(projected - 0.5 * jnp.sum(scaled * scaled, axis=-1, keepdims=True))


def layer_norm(residual, scale_row, shift_row):
    centered = residual - jnp.mean(residual, axis=-1, keepdims=True)
    variance = jnp.mean(centered * centered, axis=-1, keepdims=True)
    return centered * lax.rsqrt(variance + eps) * scale_row + shift_row


def exact_gelu(hidden):
    return jax.nn.gelu(hidden, approximate=False)


def attend_head(same_row, query_phi, key_phi, bias_row):
    length = query_phi.shape[0]
    scores = jnp.einsum("if,jf->ij", query_phi, key_phi, preferred_element_type=jnp.float32)
    coupling = toeplitz_from(jnp.exp(bias_row), length) * same_row
    weights = coupling * scores
    totals = jnp.sum(weights, axis=1, keepdims=True)
    return (weights, totals, coupling)


def mix_head(same_row, head_in):
    query_phi, key_phi, value_head, bias_row = head_in
    weights, totals, coupling = attend_head(same_row, query_phi, key_phi, bias_row)
    prob_low = (weights / totals).astype(jnp.bfloat16)
    return jnp.einsum("ij,jd->id", prob_low, value_head, preferred_element_type=jnp.float32)


def head_backward(same_row, head_in):
    query_phi, key_phi, value_head, bias_row, grad_mix = head_in
    length = query_phi.shape[0]
    weights, totals, coupling = attend_head(same_row, query_phi, key_phi, bias_row)
    shares = weights / totals
    prob_low = shares.astype(jnp.bfloat16)
    grad_probs = jnp.einsum("id,jd->ij", grad_mix, value_head, preferred_element_type=jnp.float32)
    grad_value = jnp.einsum("ij,id->jd", prob_low, grad_mix, preferred_element_type=jnp.float32)
    inner_sum = jnp.sum(grad_probs * shares, axis=1, keepdims=True)
    grad_weights = (grad_probs - inner_sum) / totals
    grad_bias = diagonal_sums(grad_weights * weights, length)
    grad_scores = (grad_weights * coupling).astype(jnp.bfloat16)
    grad_query_phi = jnp.einsum(
        "ij,jf->if", grad_scores, key_phi, preferred_element_type=jnp.float32
    )
    grad_key_phi = jnp.einsum(
        "ij,if->jf", grad_scores, query_phi, preferred_element_type=jnp.float32
    )
    return (grad_query_phi, grad_key_phi, grad_value, grad_bias)


def per_device(
    tokens,
    block_row,
    block_live,
    query_weight,
    key_weight,
    value_weight,
    out_weight,
    position_bias,
    features,
    up_weight,
    up_bias,
    down_weight,
    down_bias,
    gain_one,
    shift_one,
    gain_two,
    shift_two,
    cotangent,
):
    length = tokens.shape[0]
    head_count = position_bias.shape[0]
    head_size = features.shape[0]
    head_shape = (length, head_count, head_size)
    row_ids, live_tok = token_masks(block_row, block_live, BLK)
    same_row = (row_ids[:, None] == row_ids[None, :]).astype(jnp.float32) * live_tok[None, :]
    query_full, key_full, value_full, out_full = (
        lax.all_gather(query_weight.astype(jnp.bfloat16), ("batch", "wide"), axis=0, tiled=True),
        lax.all_gather(key_weight.astype(jnp.bfloat16), ("batch", "wide"), axis=0, tiled=True),
        lax.all_gather(value_weight.astype(jnp.bfloat16), ("batch", "wide"), axis=0, tiled=True),
        lax.all_gather(out_weight.astype(jnp.bfloat16), ("batch", "wide"), axis=0, tiled=True),
    )
    up_rows, down_rows = (
        lax.all_gather(up_weight.astype(jnp.bfloat16), "batch", axis=0, tiled=True),
        lax.all_gather(down_weight.astype(jnp.bfloat16), "batch", axis=0, tiled=True),
    )
    queries = jnp.dot(tokens, query_full, preferred_element_type=jnp.float32)
    key_rows = jnp.dot(tokens, key_full, preferred_element_type=jnp.float32)
    values = jnp.dot(tokens, value_full, preferred_element_type=jnp.float32).astype(jnp.bfloat16)
    map_features = partial(feature_map, features=features)
    query_map, query_back = jax.vjp(map_features, queries.reshape(head_shape))
    key_map, key_back = jax.vjp(map_features, key_rows.reshape(head_shape))
    query_phi = jnp.swapaxes(query_map.astype(jnp.bfloat16), 0, 1)
    key_phi = jnp.swapaxes(key_map.astype(jnp.bfloat16), 0, 1)
    value_heads = jnp.swapaxes(values.reshape(head_shape), 0, 1)
    mixed_heads = lax.map(
        partial(mix_head, same_row), (query_phi, key_phi, value_heads, position_bias)
    )
    mixed_low = jnp.swapaxes(mixed_heads, 0, 1).reshape(length, -1).astype(jnp.bfloat16)
    attention = jnp.dot(mixed_low, out_full, preferred_element_type=jnp.float32)
    residual_one = tokens.astype(jnp.float32) + attention
    normed_one, norm_one_back = jax.vjp(layer_norm, residual_one, gain_one, shift_one)
    normed_low = normed_one.astype(jnp.bfloat16)
    wide_index = lax.axis_index("wide")
    hidden_width = up_rows.shape[1]
    bias_part = lax.dynamic_slice_in_dim(up_bias, wide_index * hidden_width, hidden_width, 0)
    group_rows = lax.all_gather(normed_low, "wide", axis=0, tiled=True)
    hidden = jnp.dot(group_rows, up_rows, preferred_element_type=jnp.float32) + bias_part
    activation_full, gelu_back = jax.vjp(exact_gelu, hidden)
    activation = activation_full.astype(jnp.bfloat16)
    block_rows = activation
    branch = (
        lax.psum_scatter(
            lax.dot_general(
                block_rows, down_rows, cols_contract, preferred_element_type=jnp.float32
            ).astype(jnp.bfloat16),
            "wide",
            scatter_dimension=0,
            tiled=True,
        ).astype(jnp.float32)
        + down_bias
    )
    residual_two = normed_one + branch
    normed_two, norm_two_back = jax.vjp(layer_norm, residual_two, gain_two, shift_two)
    out_tokens = (normed_two * live_tok[:, None]).astype(jnp.bfloat16)
    grad_out = cotangent.astype(jnp.float32) * live_tok[:, None]
    grad_two, grad_gain_two, grad_shift_two = norm_two_back(grad_out)
    grad_branch = grad_two.astype(jnp.bfloat16)
    grad_down_bias = jnp.sum(grad_branch, axis=0, dtype=jnp.float32)
    group_grads = lax.all_gather(grad_branch, "wide", axis=0, tiled=True)
    grad_act = jnp.dot(group_grads, down_rows, preferred_element_type=jnp.float32)
    grad_hidden = gelu_back(grad_act)[0].astype(jnp.bfloat16)
    grad_up_part = lax.dot_general(
        group_rows, grad_hidden, rows_contract, preferred_element_type=jnp.float32
    )
    grad_down_part = lax.dot_general(
        group_grads, activation, rows_contract, preferred_element_type=jnp.float32
    )
    bias_sum = jnp.sum(grad_hidden, axis=0, dtype=jnp.float32)
    bias_grad = lax.dynamic_update_slice_in_dim(
        jnp.zeros(up_bias.shape, jnp.float32), bias_sum, wide_index * hidden_width, 0
    )
    block_rows = grad_hidden
    grad_back = lax.psum_scatter(
        lax.dot_general(
            block_rows, up_rows, cols_contract, preferred_element_type=jnp.float32
        ).astype(jnp.bfloat16),
        "wide",
        scatter_dimension=0,
        tiled=True,
    ).astype(jnp.float32)
    grad_back, grad_up_part, grad_down_part, grad_up_bias = (
        grad_back,
        grad_up_part,
        grad_down_part,
        bias_grad,
    )
    grad_up_weight, grad_down_weight = (
        lax.psum_scatter(
            grad_up_part.astype(jnp.bfloat16), "batch", scatter_dimension=0, tiled=True
        ).astype(jnp.float32),
        lax.psum_scatter(
            grad_down_part.astype(jnp.bfloat16), "batch", scatter_dimension=0, tiled=True
        ).astype(jnp.float32),
    )
    grad_one, grad_gain_one, grad_shift_one = norm_one_back(grad_two + grad_back)
    grad_attention = grad_one.astype(jnp.bfloat16)
    grad_out_local = lax.dot_general(
        mixed_low, grad_attention, rows_contract, preferred_element_type=jnp.float32
    )
    grad_mixed = lax.dot_general(
        grad_attention, out_full, cols_contract, preferred_element_type=jnp.float32
    ).astype(jnp.bfloat16)
    grad_mixed_heads = jnp.swapaxes(grad_mixed.reshape(head_shape), 0, 1)
    grad_query_phi, grad_key_phi, grad_value_heads, grad_bias_local = lax.map(
        partial(head_backward, same_row),
        (query_phi, key_phi, value_heads, position_bias, grad_mixed_heads),
    )
    grad_queries = (
        query_back(jnp.swapaxes(grad_query_phi, 0, 1))[0].reshape(length, -1).astype(jnp.bfloat16)
    )
    grad_keys = (
        key_back(jnp.swapaxes(grad_key_phi, 0, 1))[0].reshape(length, -1).astype(jnp.bfloat16)
    )
    grad_values = jnp.swapaxes(grad_value_heads, 0, 1).reshape(length, -1).astype(jnp.bfloat16)
    grad_query_local = lax.dot_general(
        tokens, grad_queries, rows_contract, preferred_element_type=jnp.float32
    )
    grad_key_local = lax.dot_general(
        tokens, grad_keys, rows_contract, preferred_element_type=jnp.float32
    )
    grad_value_local = lax.dot_general(
        tokens, grad_values, rows_contract, preferred_element_type=jnp.float32
    )
    grad_query_weight, grad_key_weight, grad_value_weight, grad_out_weight = (
        lax.psum_scatter(grad_query_local, ("batch", "wide"), scatter_dimension=0, tiled=True),
        lax.psum_scatter(grad_key_local, ("batch", "wide"), scatter_dimension=0, tiled=True),
        lax.psum_scatter(grad_value_local, ("batch", "wide"), scatter_dimension=0, tiled=True),
        lax.psum_scatter(grad_out_local, ("batch", "wide"), scatter_dimension=0, tiled=True),
    )
    grad_tokens = (
        grad_one
        + lax.dot_general(
            grad_queries, query_full, cols_contract, preferred_element_type=jnp.float32
        )
        + lax.dot_general(grad_keys, key_full, cols_contract, preferred_element_type=jnp.float32)
        + lax.dot_general(
            grad_values, value_full, cols_contract, preferred_element_type=jnp.float32
        )
    )
    (
        grad_up_bias,
        grad_down_bias,
        grad_gain_one,
        grad_shift_one,
        grad_gain_two,
        grad_shift_two,
        grad_position_bias,
    ) = lax.psum(
        (
            grad_up_bias,
            grad_down_bias,
            grad_gain_one,
            grad_shift_one,
            grad_gain_two,
            grad_shift_two,
            grad_bias_local,
        ),
        ("batch", "wide"),
    )
    return (
        out_tokens,
        grad_tokens,
        grad_query_weight,
        grad_key_weight,
        grad_value_weight,
        grad_out_weight,
        grad_position_bias,
        grad_up_weight,
        grad_up_bias,
        grad_down_weight,
        grad_down_bias,
        grad_gain_one,
        grad_shift_one,
        grad_gain_two,
        grad_shift_two,
    )


def solution(mesh):
    placed = (
        P(("batch", "wide"), None),
        P(("batch", "wide")),
        P(("batch", "wide")),
        P(("batch", "wide"), None),
        P(("batch", "wide"), None),
        P(("batch", "wide"), None),
        P(("batch", "wide"), None),
        P(),
        P(),
        P("batch", "wide"),
        P(),
        P("batch", "wide"),
        P(),
        P(),
        P(),
        P(),
        P(),
        P(("batch", "wide"), None),
    )
    return jax.shard_map(
        per_device,
        mesh=mesh,
        in_specs=placed,
        out_specs=(
            P(("batch", "wide"), None),
            P(("batch", "wide"), None),
            P(("batch", "wide"), None),
            P(("batch", "wide"), None),
            P(("batch", "wide"), None),
            P(("batch", "wide"), None),
            P(),
            P("batch", "wide"),
            P(),
            P("batch", "wide"),
            P(),
            P(),
            P(),
            P(),
            P(),
        ),
        check_vma=False,
    )
```

profile of v0, /device:TPU:0, one launch (start us, length us, event | category | flops | bytes accessed | tf_op | source)
XLA Modules:
  0.0 1346.2 jit_solution(8290527931595110936)
XLA Ops:
  16.6 51.7 %all-gather.11.cloned.1.call-done = bf16[768,768]{1,0:T(8,128)(2,1)} async-done(((bf16[24,768]{1,0:T(8,128)(2,1)}), bf16[768,768]{1,0:T(8,128)(2,1)}) %all-gather.11.cloned.1.call-update) | async-done | bytes 1179664 | tf_op jit(solution)/shard_map/all_gather | solution.py:116
  68.3 3.7 broadcast_multiply_fusion
  80.4 44.4 %all-gather.9.cloned.1.call-done = bf16[768,768]{1,0:T(8,128)(2,1)} async-done(((bf16[24,768]{1,0:T(8,128)(2,1)}), bf16[768,768]{1,0:T(8,128)(2,1)}) %all-gather.9.cloned.1.call-update) | async-done | bytes 1179664 | tf_op jit(solution)/shard_map/all_gather | solution.py:115
  124.7 3.8 broadcast_multiply_fusion.1
  137.0 44.3 %all-gather.13.cloned.1.call-done = bf16[768,768]{1,0:T(8,128)(2,1)} async-done(((bf16[24,768]{1,0:T(8,128)(2,1)}), bf16[768,768]{1,0:T(8,128)(2,1)}) %all-gather.13.cloned.1.call-update) | async-done | bytes 1179664 | tf_op jit(solution)/shard_map/all_gather | solution.py:117
  185.1 113.5 %while.30 = (s32[]{:T(128)}, bf16[12,512,64]{1,2,0:T(8,128)(2,1)}, f32[12,1024]{1,0:T(8,128)}, bf16[12,512,64]{2,1,0:T(8,128)(2,1)}, bf16[12,512,64]{2,1,0:T(8,1...) while((s32[]{:T(128)}, bf16[12,512,64]{1,2,0:T(8,128)(2,1)}, ...), condition=%wide.region_4.5_spmd.clone.clone, body=%wide.region_2.4_spmd.clone.sunk.clone | while | flops 68943360 | bytes 18378840 | solution.py:133
  304.7 25.9 %all-gather.17.cloned.1.call-done = bf16[2048,768]{1,0:T(8,128)(2,1)} async-done(((bf16[512,768]{1,0:T(8,128)(2,1)}), bf16[2048,768]{1,0:T(8,128)(2,1)}) %all-gather.17.cloned.1.call-update) | async-done | bytes 3145744 | tf_op jit(solution)/shard_map/all_gather | solution.py:144
  330.6 18.9 %multiply_convert_fusion.1 = (bf16[2048,768]{1,0:T(8,128)(2,1)}, f32[2048,768]{1,0:T(8,128)}, f32[2048,768]{1,0:T(8,128)}) fusion(f32[768]{0:T(1024)S(1)} %dynamic_slice.32, bf16[2048,768]{1,0:T(8,128)(2,1)} %all-gather.17.cloned.1.call-done, bf16[768,768]{1,0:T(8,128)(2,1)} %all-gather.19.cloned.1.call-done), kind=kOutput, calls=%fused_computation.59 | convolution fusion | flops 2519728128 | bytes 20057088 | tf_op jit(solution)/shard_map/dot_general | solution.py:145
  349.5 25.0 %all-gather.21.cloned.1.call-done = bf16[768,768]{1,0:T(8,128)(2,1)} async-done(((bf16[96,768]{1,0:T(8,128)(2,1)}), bf16[768,768]{1,0:T(8,128)(2,1)}) %all-gather.21.cloned.1.call-update) | async-done | bytes 1179664 | tf_op jit(solution)/shard_map/all_gather | solution.py:122
  374.4 6.5 convolution_convert_fusion.1
  381.1 36.8 %reduce-scatter.15.cloned.1.call-done = bf16[512,768]{1,0:T(8,128)(2,1)} async-done(((bf16[2048,768]{1,0:T(8,128)(2,1)}), bf16[512,768]{1,0:T(8,128)(2,1)}) %reduce-scatter.15.cloned.1.call-update) | async-done | bytes 786448 | tf_op jit(solution)/shard_map/reduce_scatter | solution.py:150
  425.8 28.4 %all-gather.23.cloned.1.call-done = bf16[2048,768]{1,0:T(8,128)(2,1)} async-done(((bf16[512,768]{1,0:T(8,128)(2,1)}), bf16[2048,768]{1,0:T(8,128)(2,1)}) %all-gather.23.cloned.1.call-update) | async-done | bytes 3145744 | tf_op jit(solution)/shard_map/all_gather | solution.py:167
  454.2 10.6 convert_reduce_fusion
  466.4 4.0 convolution_convert_fusion
  470.5 6.5 convolution_convert_fusion.2
  477.5 7.4 convolution_convert_fusion.3
  485.3 23.3 %reduce-scatter.17.cloned.1.call-done = bf16[512,768]{1,0:T(8,128)(2,1)} async-done(((bf16[2048,768]{1,0:T(8,128)(2,1)}), bf16[512,768]{1,0:T(8,128)(2,1)}) %reduce-scatter.17.cloned.1.call-update) | async-done | bytes 786448 | tf_op jit(solution)/shard_map/reduce_scatter | solution.py:181
  515.3 272.2 %while.31 = (s32[]{:T(128)}, f32[12,512,64]{1,2,0:T(8,128)}, f32[12,512,64]{1,2,0:T(8,128)}, bf16[12,512,64]{1,2,0:T(8,128)(2,1)}, f32[12,1024]{1,0:T(8,128)}, /...) while((s32[]{:T(128)}, f32[12,512,64]{1,2,0:T(8,128)}, ...), condition=%wide.region_19.20_spmd.clone.clone, body=%wide.region_15.0_spmd.clone.sunk.clone | while | flops 173013504 | bytes 51068068 | solution.py:212
  527.3 3.2 reshape.226
  550.0 3.2 reshape.226
  572.8 3.2 reshape.226
  618.2 3.2 reshape.226
  640.8 3.2 reshape.226
  663.5 3.2 reshape.226
  787.6 4.0 fusion.68
  795.0 3.5 fusion.56
  810.1 3.9 fusion.50
  833.1 78.5 %all-reduce.5.cloned.1.call-done = (f32[12,1024]{1,0:T(8,128)}, f32[3072]{0:T(1024)}, f32[768]{0:T(1024)}, f32[768]{0:T(1024)}, f32[768]{0:T(1024)}, /*index=5*/f32[768]{0:T(1024)}, f32[768]{0:T(1024)}) async-done(((f32[12,1024]{1,0:T(8,128)}, f32[3072]{0:T(1024)}, f32[768]{0:T(1024)}, f32[768]{0:T(1024)}, f32[768]{0:T(1024)}, /*index=5*/f32[768]{0:T(1024)}, f32[768]{0:T(1024)}), (f32[12,1024]{1,0:T(8,128)}, ...) | async-done | bytes 76816 | tf_op jit(solution)/shard_map/psum | solution.py:256
  911.5 105.9 %reduce-scatter.19.cloned.1.call-done = f32[24,768]{1,0:T(8,128)} async-done(((f32[768,768]{1,0:T(8,128)}), f32[24,768]{1,0:T(8,128)}) %reduce-scatter.19.cloned.1.call-update) | async-done | bytes 73744 | tf_op jit(solution)/shard_map/reduce_scatter | solution.py:236
  1017.5 104.5 %reduce-scatter.25.cloned.1.call-done = f32[24,768]{1,0:T(8,128)} async-done(((f32[768,768]{1,0:T(8,128)}), f32[24,768]{1,0:T(8,128)}) %reduce-scatter.25.cloned.1.call-update) | async-done | bytes 73744
  1122.0 103.8 %reduce-scatter.27.cloned.1.call-done = f32[24,768]{1,0:T(8,128)} async-done(((f32[768,768]{1,0:T(8,128)}), f32[24,768]{1,0:T(8,128)}) %reduce-scatter.27.cloned.1.call-update) | async-done | bytes 73744
  1225.8 104.5 %reduce-scatter.29.cloned.1.call-done = f32[24,768]{1,0:T(8,128)} async-done(((f32[768,768]{1,0:T(8,128)}), f32[24,768]{1,0:T(8,128)}) %reduce-scatter.29.cloned.1.call-update) | async-done | bytes 73744
  (568 shorter events, 461.2 us)
Async XLA Ops:
  7.2 67.6 %copy-start = (f32[64,64]{1,0:T(8,128)S(1)}, f32[64,64]{1,0:T(8,128)}, u32[]{:S(2)}) copy-start(f32[64,64]{1,0:T(8,128)} %param.30) | copy-start | bytes 49156
  7.2 8.2 copy-start.30
  7.2 61.1 %all-gather.11.cloned.1.call-start = ((), (), s32[]{:S(2)}) async-start(), calls=%async_computation.9 | async-start | bytes 1216512 | tf_op jit(solution)/shard_map/all_gather | solution.py:116
  8.8 116.0 %all-gather.9.cloned.1.call-start = ((), (), s32[]{:S(2)}) async-start(), calls=%async_computation.8 | async-start | bytes 1216512 | tf_op jit(solution)/shard_map/all_gather | solution.py:115
  10.4 170.9 %all-gather.13.cloned.1.call-start = ((), (), s32[]{:S(2)}) async-start(), calls=%async_computation.10 | async-start | bytes 1216512 | tf_op jit(solution)/shard_map/all_gather | solution.py:117
  11.9 4.6 copy-start.31
  11.9 56.4 %copy-start.2 = (bf16[512,768]{1,0:T(8,128)(2,1)S(1)}, bf16[512,768]{1,0:T(8,128)(2,1)}, u32[]{:S(2)}) copy-start(bf16[512,768]{1,0:T(8,128)(2,1)} %param.22) | copy-start | bytes 2359300
  12.0 286.7 %all-gather.15.cloned.1.call-start = ((), (), s32[]{:S(2)}) async-start(), calls=%async_computation.11 | async-start | bytes 1216512 | tf_op jit(solution)/shard_map/all_gather | solution.py:118
  13.6 291.1 %all-gather.19.cloned.1.call-start = ((), (), s32[]{:S(2)}) async-start(), calls=%async_computation.13 | async-start | bytes 1327104 | tf_op jit(solution)/shard_map/all_gather | solution.py:121
  15.3 315.3 %all-gather.17.cloned.1.call-start = ((), (), s32[]{:S(2)}) async-start(), calls=%async_computation.12 | async-start | bytes 3932160 | tf_op jit(solution)/shard_map/all_gather | solution.py:144
  15.4 56.6 %copy-start.8 = (bf16[12,512,64]{1,2,0:T(8,128)(2,1)}, bf16[12,512,64]{1,2,0:T(8,128)(2,1)S(1)}, u32[]{:S(2)}) copy-start(bf16[12,512,64]{1,2,0:T(8,128)(2,1)S(1)} %fusion.76) | copy-start | bytes 2359300
  302.9 71.5 %all-gather.21.cloned.1.call-start = ((), (), s32[]{:S(2)}) async-start(), calls=%async_computation.14 | async-start | bytes 1327104 | tf_op jit(solution)/shard_map/all_gather | solution.py:122
  303.7 114.2 %reduce-scatter.15.cloned.1.call-start = ((), (), s32[]{:S(2)}) async-start(), calls=%async_computation.15 | async-start | bytes 3932160 | tf_op jit(solution)/shard_map/reduce_scatter | solution.py:150
  381.0 36.9 %copy-start.28 = (f32[768]{0:T(1024)S(1)}, f32[768]{0:T(1024)}, u32[]{:S(2)}) copy-start(f32[768]{0:T(1024)} %param.34) | copy-start | bytes 9220
  381.0 73.2 %all-gather.23.cloned.1.call-start = ((), (), s32[]{:S(2)}) async-start(), calls=%async_computation.16 | async-start | bytes 3932160 | tf_op jit(solution)/shard_map/all_gather | solution.py:167
  425.5 83.1 %reduce-scatter.17.cloned.1.call-start = ((), (), s32[]{:S(2)}) async-start(), calls=%async_computation.17 | async-start | bytes 3932160 | tf_op jit(solution)/shard_map/reduce_scatter | solution.py:181
  454.2 12.3 copy-start.33
  470.5 353.7 %reduce-scatter.23.cloned.1.call-start = ((), (), s32[]{:S(2)}) async-start(), calls=%async_computation.20 | async-start | bytes 1327104 | tf_op jit(solution)/shard_map/reduce_scatter | solution.py:199
  477.1 348.9 %reduce-scatter.21.cloned.1.call-start = ((), (), s32[]{:S(2)}) async-start(), calls=%async_computation.19 | async-start | bytes 1327104 | tf_op jit(solution)/shard_map/reduce_scatter | solution.py:196
  477.5 7.4 copy-start.25
  484.9 426.7 %all-reduce.5.cloned.1.call-start = ((), (), s32[]{:S(2)}) async-start(), calls=%async_computation.24 | async-start | bytes 196608 | tf_op jit(solution)/shard_map/psum | solution.py:256
  787.5 229.9 %reduce-scatter.19.cloned.1.call-start = ((), (), s32[]{:S(2)}) async-start(), calls=%async_computation.18 | async-start | bytes 2433024 | tf_op jit(solution)/shard_map/reduce_scatter | solution.py:236
  791.6 330.4 %reduce-scatter.25.cloned.1.call-start = ((), (), s32[]{:S(2)}) async-start(), calls=%async_computation.21 | async-start | bytes 2433024
  791.8 3.2 copy-start.6
  791.8 3.2 copy-start.21
  795.0 3.5 copy-start.7
  795.0 3.5 copy-start.10
  795.0 3.8 copy-start.11
  807.0 418.8 %reduce-scatter.27.cloned.1.call-start = ((), (), s32[]{:S(2)}) async-start(), calls=%async_computation.22 | async-start | bytes 2433024
  817.7 512.6 %reduce-scatter.29.cloned.1.call-start = ((), (), s32[]{:S(2)}) async-start(), calls=%async_computation.23 | async-start | bytes 2433024
  824.1 3.5 copy-start.15
  824.1 3.5 copy-start.20
  (31 other events, 46.9 us)
Sparse Core Ops, SparseCore 0:
  11.5 56.7 all-gather.10
  71.7 52.9 all-gather.8
  128.2 52.9 all-gather.12
  184.6 52.9 all-gather.14
  240.2 39.9 all-gather.18
  303.1 27.4 all-gather.16
  333.3 41.0 all-gather.20
  381.1 36.7 reduce-scatter.14
  425.6 28.5 all-gather.22
  470.6 37.9 reduce-scatter.16
  512.0 64.1 reduce-scatter.22
  579.4 63.0 reduce-scatter.20
  787.7 123.8 all-reduce.4
  917.3 100.1 reduce-scatter.18
  1024.0 97.9 reduce-scatter.24
  1127.7 98.0 reduce-scatter.26
  1232.4 97.9 reduce-scatter.28
where the time goes:
time: 1360 us; the launch traced here: 1350 us
  waiting for transfers between devices  777 us (57%)
  local copies, waits for them, and re-layouts  285 us (21%)
  matrix products  231 us (17%)
  other arithmetic  34.5 us (3%)
  between operations  14.6 us (1%)
    unnamed x20, waiting for transfers between devices  313 us
    reduce_scatter x1, waiting for transfers between devices, per_device(): lax.psum_scatter(grad_out_local, ('batch', 'wide'), scatter_dimension=0,...  106 us
    psum x1, waiting for transfers between devices, per_device(): lax.psum((grad_up_bias, grad_down_bias, grad_gain_one, grad_shift_one, gr...  78.5 us
    reshape x24, local copies, waits for them, and re-layouts, toeplitz_from(): tiled_flat[:length * (2 * length - 1)].reshape(length, 2 * length - 1)  66.9 us
    all_gather x1, waiting for transfers between devices, per_device(): lax.all_gather(key_weight.astype(jnp.bfloat16), ('batch', 'wide'), axis=0...  51.7 us
    all_gather x1, waiting for transfers between devices, per_device(): lax.all_gather(query_weight.astype(jnp.bfloat16), ('batch', 'wide'), axis...  44.4 us
    all_gather x1, waiting for transfers between devices, per_device(): lax.all_gather(value_weight.astype(jnp.bfloat16), ('batch', 'wide'), axis...  44.3 us
    slice x24, local copies, waits for them, and re-layouts, toeplitz_from(): tiled_flat[:length * (2 * length - 1)].reshape(length, 2 * length - 1)  39.7 us
  transfers between devices with their start and end apart: 17, of which 13 were waited for; matrix products, arithmetic and copies ran while one was open for 37% of the time, Pallas kernels for 0%

commit v1 on v0

--- a/solution.py
+++ b/solution.py
@@ -254,16 +254,19 @@
         grad_shift_two,
         grad_position_bias,
     ) = lax.psum(
-        (
-            grad_up_bias,
-            grad_down_bias,
-            grad_gain_one,
-            grad_shift_one,
-            grad_gain_two,
-            grad_shift_two,
-            grad_bias_local,
+        lax.psum(
+            (
+                grad_up_bias,
+                grad_down_bias,
+                grad_gain_one,
+                grad_shift_one,
+                grad_gain_two,
+                grad_shift_two,
+                grad_bias_local,
+            ),
+            "wide",
         ),
-        ("batch", "wide"),
+        "batch",
     )
     return (
         out_tokens,

time: 1360 us -> 1480 us (1.088)
  waiting for transfers between devices: 777 us -> 892 us
    psum x0 -> x1, waiting for transfers between devices: none -> 67.4 us  [per_device(): lax.psum(lax.psum((grad_up_bias, grad_down_bias, grad_gain_one, grad_shif...]
    reduce_scatter x1, waiting for transfers between devices: 0.01 us -> 65.2 us  [per_device(): lax.psum_scatter(grad_up_part.astype(jnp.bfloat16), 'batch', scatter_dime...]
    psum x1, waiting for transfers between devices: 78.5 us -> 18.6 us  [per_device(): lax.psum((grad_up_bias, grad_down_bias, grad_gain_one, grad_shift_one, gr...]
    reduce_scatter x1, waiting for transfers between devices: 0.02 us -> 29.3 us  [per_device(): lax.psum_scatter(grad_down_part.astype(jnp.bfloat16), 'batch', scatter_di...]
    unnamed x20 -> x21, waiting for transfers between devices: 313 us -> 313 us
    unnamed x82 -> x80, local copies, waits for them, and re-layouts: 33.6 us -> 33.5 us
  transfers between devices with their start and end apart: 17 -> 18, of which waited for: 13 -> 16; matrix products, arithmetic and copies ran while one was open for 37% -> 16% of each run, Pallas kernels for 0% -> 0%
where the time goes in v1:
time: 1480 us; the launch traced here: 1460 us
  waiting for transfers between devices  892 us (60%)
  local copies, waits for them, and re-layouts  285 us (19%)
  matrix products  232 us (16%)
  other arithmetic  34.9 us (2%)
  between operations  15.2 us (1%)
    unnamed x21, waiting for transfers between devices  313 us
    reduce_scatter x1, waiting for transfers between devices, per_device(): lax.psum_scatter(grad_out_local, ('batch', 'wide'), scatter_dimension=0,...  105 us
    psum x1, waiting for transfers between devices, per_device(): lax.psum(lax.psum((grad_up_bias, grad_down_bias, grad_gain_one, grad_shif...  67.4 us
    reshape x24, local copies, waits for them, and re-layouts, toeplitz_from(): tiled_flat[:length * (2 * length - 1)].reshape(length, 2 * length - 1)  67.1 us
    reduce_scatter x1, waiting for transfers between devices, per_device(): lax.psum_scatter(grad_up_part.astype(jnp.bfloat16), 'batch', scatter_dime...  65.2 us
    all_gather x1, waiting for transfers between devices, per_device(): lax.all_gather(key_weight.astype(jnp.bfloat16), ('batch', 'wide'), axis=0...  51.7 us
    all_gather x1, waiting for transfers between devices, per_device(): lax.all_gather(query_weight.astype(jnp.bfloat16), ('batch', 'wide'), axis...  44.4 us
    all_gather x1, waiting for transfers between devices, per_device(): lax.all_gather(value_weight.astype(jnp.bfloat16), ('batch', 'wide'), axis...  44.3 us
  transfers between devices with their start and end apart: 18, of which 16 were waited for; matrix products, arithmetic and copies ran while one was open for 16% of the time, Pallas kernels for 0%

profile of v1, /device:TPU:0, one launch (start us, length us, event | category | flops | bytes accessed | tf_op | source)
XLA Modules:
  0.0 1463.1 jit_solution(5220341674289912776)
XLA Ops:
  16.6 51.7 %all-gather.11.cloned.1.call-done = bf16[768,768]{1,0:T(8,128)(2,1)} async-done(((bf16[24,768]{1,0:T(8,128)(2,1)}), bf16[768,768]{1,0:T(8,128)(2,1)}) %all-gather.11.cloned.1.call-update) | async-done | bytes 1179664 | tf_op jit(solution)/shard_map/all_gather | solution.py:116
  68.3 3.7 broadcast_multiply_fusion
  80.4 44.4 %all-gather.9.cloned.1.call-done = bf16[768,768]{1,0:T(8,128)(2,1)} async-done(((bf16[24,768]{1,0:T(8,128)(2,1)}), bf16[768,768]{1,0:T(8,128)(2,1)}) %all-gather.9.cloned.1.call-update) | async-done | bytes 1179664 | tf_op jit(solution)/shard_map/all_gather | solution.py:115
  124.7 3.8 broadcast_multiply_fusion.1
  137.0 44.3 %all-gather.13.cloned.1.call-done = bf16[768,768]{1,0:T(8,128)(2,1)} async-done(((bf16[24,768]{1,0:T(8,128)(2,1)}), bf16[768,768]{1,0:T(8,128)(2,1)}) %all-gather.13.cloned.1.call-update) | async-done | bytes 1179664 | tf_op jit(solution)/shard_map/all_gather | solution.py:117
  185.1 113.5 %while.30 = (s32[]{:T(128)}, bf16[12,512,64]{1,2,0:T(8,128)(2,1)}, f32[12,1024]{1,0:T(8,128)}, bf16[12,512,64]{2,1,0:T(8,128)(2,1)}, bf16[12,512,64]{2,1,0:T(8,1...) while((s32[]{:T(128)}, bf16[12,512,64]{1,2,0:T(8,128)(2,1)}, ...), condition=%wide.region_4.5_spmd.clone.clone, body=%wide.region_2.4_spmd.clone.sunk.clone | while | flops 68943360 | bytes 18378840 | solution.py:133
  304.9 25.7 %all-gather.17.cloned.1.call-done = bf16[2048,768]{1,0:T(8,128)(2,1)} async-done(((bf16[512,768]{1,0:T(8,128)(2,1)}), bf16[2048,768]{1,0:T(8,128)(2,1)}) %all-gather.17.cloned.1.call-update) | async-done | bytes 3145744 | tf_op jit(solution)/shard_map/all_gather | solution.py:144
  330.6 18.9 %multiply_convert_fusion.1 = (bf16[2048,768]{1,0:T(8,128)(2,1)}, f32[2048,768]{1,0:T(8,128)}, f32[2048,768]{1,0:T(8,128)}) fusion(f32[768]{0:T(1024)S(1)} %dynamic_slice.32, bf16[2048,768]{1,0:T(8,128)(2,1)} %all-gather.17.cloned.1.call-done, bf16[768,768]{1,0:T(8,128)(2,1)} %all-gather.19.cloned.1.call-done), kind=kOutput, calls=%fused_computation.59 | convolution fusion | flops 2519728128 | bytes 20057088 | tf_op jit(solution)/shard_map/dot_general | solution.py:145
  349.5 25.0 %all-gather.21.cloned.1.call-done = bf16[768,768]{1,0:T(8,128)(2,1)} async-done(((bf16[96,768]{1,0:T(8,128)(2,1)}), bf16[768,768]{1,0:T(8,128)(2,1)}) %all-gather.21.cloned.1.call-update) | async-done | bytes 1179664 | tf_op jit(solution)/shard_map/all_gather | solution.py:122
  374.4 6.6 convolution_convert_fusion.1
  381.1 36.8 %reduce-scatter.15.cloned.1.call-done = bf16[512,768]{1,0:T(8,128)(2,1)} async-done(((bf16[2048,768]{1,0:T(8,128)(2,1)}), bf16[512,768]{1,0:T(8,128)(2,1)}) %reduce-scatter.15.cloned.1.call-update) | async-done | bytes 786448 | tf_op jit(solution)/shard_map/reduce_scatter | solution.py:150
  425.5 28.6 %all-gather.23.cloned.1.call-done = bf16[2048,768]{1,0:T(8,128)(2,1)} async-done(((bf16[512,768]{1,0:T(8,128)(2,1)}), bf16[2048,768]{1,0:T(8,128)(2,1)}) %all-gather.23.cloned.1.call-update) | async-done | bytes 3145744 | tf_op jit(solution)/shard_map/all_gather | solution.py:167
  454.2 10.6 convert_reduce_fusion
  466.4 4.1 convolution_convert_fusion
  471.1 37.5 %reduce-scatter.17.cloned.1.call-done = bf16[512,768]{1,0:T(8,128)(2,1)} async-done(((bf16[2048,768]{1,0:T(8,128)(2,1)}), bf16[512,768]{1,0:T(8,128)(2,1)}) %reduce-scatter.17.cloned.1.call-update) | async-done | bytes 786448 | tf_op jit(solution)/shard_map/reduce_scatter | solution.py:181
  515.3 272.7 %while.31 = (s32[]{:T(128)}, f32[12,512,64]{1,2,0:T(8,128)}, f32[12,512,64]{1,2,0:T(8,128)}, bf16[12,512,64]{1,2,0:T(8,128)(2,1)}, f32[12,1024]{1,0:T(8,128)}, /...) while((s32[]{:T(128)}, f32[12,512,64]{1,2,0:T(8,128)}, ...), condition=%wide.region_19.20_spmd.clone.clone, body=%wide.region_15.0_spmd.clone.sunk.clone | while | flops 173013504 | bytes 51068068 | solution.py:212
  527.3 3.2 reshape.226
  572.7 3.2 reshape.226
  686.3 3.2 reshape.226
  709.0 3.2 reshape.226
  788.2 6.5 convolution_convert_fusion.2
  794.8 6.6 convolution_convert_fusion.3
  801.5 18.6 %all-reduce.9.cloned.1.call-done = (f32[12,1024]{1,0:T(8,128)}, f32[3072]{0:T(1024)}, f32[768]{0:T(1024)}, f32[768]{0:T(1024)}, f32[768]{0:T(1024)}, /*index=5*/f32[768]{0:T(1024)}, f32[768]{0:T(1024)}) async-done(((f32[12,1024]{1,0:T(8,128)}, f32[3072]{0:T(1024)}, f32[768]{0:T(1024)}, f32[768]{0:T(1024)}, f32[768]{0:T(1024)}, /*index=5*/f32[768]{0:T(1024)}, f32[768]{0:T(1024)}), (f32[12,1024]{1,0:T(8,128)}, ...) | async-done | bytes 76816 | tf_op jit(solution)/shard_map/psum | solution.py:257
  825.7 3.9 fusion.56
  841.6 4.4 fusion.50
  858.6 29.3 %reduce-scatter.23.cloned.1.call-done = bf16[96,768]{1,0:T(8,128)(2,1)} async-done(((bf16[768,768]{1,0:T(8,128)(2,1)}), bf16[96,768]{1,0:T(8,128)(2,1)}) %reduce-scatter.23.cloned.1.call-update) | async-done | bytes 147472 | tf_op jit(solution)/shard_map/reduce_scatter | solution.py:199
  889.6 65.2 %reduce-scatter.21.cloned.1.call-done = bf16[96,768]{1,0:T(8,128)(2,1)} async-done(((bf16[768,768]{1,0:T(8,128)(2,1)}), bf16[96,768]{1,0:T(8,128)(2,1)}) %reduce-scatter.21.cloned.1.call-update) | async-done | bytes 147472 | tf_op jit(solution)/shard_map/reduce_scatter | solution.py:196
  962.2 67.4 %all-reduce.7.cloned.1.call-done = (f32[12,1024]{1,0:T(8,128)}, f32[3072]{0:T(1024)}, f32[768]{0:T(1024)}, f32[768]{0:T(1024)}, f32[768]{0:T(1024)}, /*index=5*/f32[768]{0:T(1024)}, f32[768]{0:T(1024)}) async-done(((f32[12,1024]{1,0:T(8,128)}, f32[3072]{0:T(1024)}, f32[768]{0:T(1024)}, f32[768]{0:T(1024)}, f32[768]{0:T(1024)}, /*index=5*/f32[768]{0:T(1024)}, f32[768]{0:T(1024)}), (f32[12,1024]{1,0:T(8,128)}, ...) | async-done | bytes 76816 | tf_op jit(solution)/shard_map/psum | solution.py:256
  1029.6 104.7 %reduce-scatter.19.cloned.1.call-done = f32[24,768]{1,0:T(8,128)} async-done(((f32[768,768]{1,0:T(8,128)}), f32[24,768]{1,0:T(8,128)}) %reduce-scatter.19.cloned.1.call-update) | async-done | bytes 73744 | tf_op jit(solution)/shard_map/reduce_scatter | solution.py:236
  1134.4 103.8 %reduce-scatter.25.cloned.1.call-done = f32[24,768]{1,0:T(8,128)} async-done(((f32[768,768]{1,0:T(8,128)}), f32[24,768]{1,0:T(8,128)}) %reduce-scatter.25.cloned.1.call-update) | async-done | bytes 73744
  1238.1 104.6 %reduce-scatter.27.cloned.1.call-done = f32[24,768]{1,0:T(8,128)} async-done(((f32[768,768]{1,0:T(8,128)}), f32[24,768]{1,0:T(8,128)}) %reduce-scatter.27.cloned.1.call-update) | async-done | bytes 73744
  1342.8 103.9 %reduce-scatter.29.cloned.1.call-done = f32[24,768]{1,0:T(8,128)} async-done(((f32[768,768]{1,0:T(8,128)}), f32[24,768]{1,0:T(8,128)}) %reduce-scatter.29.cloned.1.call-update) | async-done | bytes 73744
  (569 shorter events, 473.0 us)
Async XLA Ops:
  7.2 67.6 %copy-start = (f32[64,64]{1,0:T(8,128)S(1)}, f32[64,64]{1,0:T(8,128)}, u32[]{:S(2)}) copy-start(f32[64,64]{1,0:T(8,128)} %param.30) | copy-start | bytes 49156
  7.2 8.2 copy-start.29
  7.2 61.1 %all-gather.11.cloned.1.call-start = ((), (), s32[]{:S(2)}) async-start(), calls=%async_computation.9 | async-start | bytes 1216512 | tf_op jit(solution)/shard_map/all_gather | solution.py:116
  8.8 116.0 %all-gather.9.cloned.1.call-start = ((), (), s32[]{:S(2)}) async-start(), calls=%async_computation.8 | async-start | bytes 1216512 | tf_op jit(solution)/shard_map/all_gather | solution.py:115
  10.4 170.9 %all-gather.13.cloned.1.call-start = ((), (), s32[]{:S(2)}) async-start(), calls=%async_computation.10 | async-start | bytes 1216512 | tf_op jit(solution)/shard_map/all_gather | solution.py:117
  11.9 4.6 copy-start.30
  11.9 56.4 %copy-start.2 = (bf16[512,768]{1,0:T(8,128)(2,1)S(1)}, bf16[512,768]{1,0:T(8,128)(2,1)}, u32[]{:S(2)}) copy-start(bf16[512,768]{1,0:T(8,128)(2,1)} %param.22) | copy-start | bytes 2359300
  12.0 286.7 %all-gather.15.cloned.1.call-start = ((), (), s32[]{:S(2)}) async-start(), calls=%async_computation.11 | async-start | bytes 1216512 | tf_op jit(solution)/shard_map/all_gather | solution.py:118
  13.6 291.3 %all-gather.19.cloned.1.call-start = ((), (), s32[]{:S(2)}) async-start(), calls=%async_computation.13 | async-start | bytes 1327104 | tf_op jit(solution)/shard_map/all_gather | solution.py:121
  15.3 315.3 %all-gather.17.cloned.1.call-start = ((), (), s32[]{:S(2)}) async-start(), calls=%async_computation.12 | async-start | bytes 3932160 | tf_op jit(solution)/shard_map/all_gather | solution.py:144
  15.4 56.6 %copy-start.7 = (bf16[12,512,64]{1,2,0:T(8,128)(2,1)}, bf16[12,512,64]{1,2,0:T(8,128)(2,1)S(1)}, u32[]{:S(2)}) copy-start(bf16[12,512,64]{1,2,0:T(8,128)(2,1)S(1)} %fusion.76) | copy-start | bytes 2359300
  303.0 71.5 %all-gather.21.cloned.1.call-start = ((), (), s32[]{:S(2)}) async-start(), calls=%async_computation.14 | async-start | bytes 1327104 | tf_op jit(solution)/shard_map/all_gather | solution.py:122
  303.7 114.1 %reduce-scatter.15.cloned.1.call-start = ((), (), s32[]{:S(2)}) async-start(), calls=%async_computation.15 | async-start | bytes 3932160 | tf_op jit(solution)/shard_map/reduce_scatter | solution.py:150
  381.0 36.9 %copy-start.27 = (f32[768]{0:T(1024)S(1)}, f32[768]{0:T(1024)}, u32[]{:S(2)}) copy-start(f32[768]{0:T(1024)} %param.34) | copy-start | bytes 9220
  381.0 73.2 %all-gather.23.cloned.1.call-start = ((), (), s32[]{:S(2)}) async-start(), calls=%async_computation.16 | async-start | bytes 3932160 | tf_op jit(solution)/shard_map/all_gather | solution.py:167
  425.5 83.1 %reduce-scatter.17.cloned.1.call-start = ((), (), s32[]{:S(2)}) async-start(), calls=%async_computation.17 | async-start | bytes 3932160 | tf_op jit(solution)/shard_map/reduce_scatter | solution.py:181
  454.2 12.2 copy-start.32
  470.5 349.6 %all-reduce.9.cloned.1.call-start = ((), (), s32[]{:S(2)}) async-start(), calls=%async_computation.25 | async-start | bytes 196608 | tf_op jit(solution)/shard_map/psum | solution.py:257
  471.0 40.2 %copy-start.24 = (f32[3072]{0:T(1024)}, f32[3072]{0:T(1024)S(1)}, u32[]{:S(2)}) copy-start(f32[3072]{0:T(1024)S(1)} %dynamic_update_slice.20) | copy-start | bytes 36868
  788.0 100.0 %reduce-scatter.23.cloned.1.call-start = ((), (), s32[]{:S(2)}) async-start(), calls=%async_computation.20 | async-start | bytes 1327104 | tf_op jit(solution)/shard_map/reduce_scatter | solution.py:199
  794.8 160.0 %reduce-scatter.21.cloned.1.call-start = ((), (), s32[]{:S(2)}) async-start(), calls=%async_computation.19 | async-start | bytes 1327104 | tf_op jit(solution)/shard_map/reduce_scatter | solution.py:196
  794.8 25.4 %copy-start.5 = (f32[512,768]{1,0:T(8,128)S(1)}, f32[512,768]{1,0:T(8,128)}, u32[]{:S(2)}) copy-start(f32[512,768]{1,0:T(8,128)} %copy-done.4) | copy-start | bytes 4718596
  801.5 18.7 %copy-start.11 = (bf16[12,512,64]{1,2,0:T(8,128)(2,1)S(1)}, bf16[12,512,64]{1,2,0:T(8,128)(2,1)}, u32[]{:S(2)}) copy-start(bf16[12,512,64]{1,2,0:T(8,128)(2,1)} %get-tuple-element.112) | copy-start | bytes 2359300
  801.5 228.1 %all-reduce.7.cloned.1.call-start = ((), (), s32[]{:S(2)}) async-start(), calls=%async_computation.24 | async-start | bytes 196608 | tf_op jit(solution)/shard_map/psum | solution.py:256
  820.1 314.2 %reduce-scatter.19.cloned.1.call-start = ((), (), s32[]{:S(2)}) async-start(), calls=%async_computation.18 | async-start | bytes 2433024 | tf_op jit(solution)/shard_map/reduce_scatter | solution.py:236
  822.5 415.6 %reduce-scatter.25.cloned.1.call-start = ((), (), s32[]{:S(2)}) async-start(), calls=%async_computation.21 | async-start | bytes 2433024
  825.7 4.0 copy-start.6
  825.7 4.0 copy-start.9
  825.7 4.2 copy-start.10
  838.2 504.5 %reduce-scatter.27.cloned.1.call-start = ((), (), s32[]{:S(2)}) async-start(), calls=%async_computation.22 | async-start | bytes 2433024
  852.2 594.5 %reduce-scatter.29.cloned.1.call-start = ((), (), s32[]{:S(2)}) async-start(), calls=%async_computation.23 | async-start | bytes 2433024
  858.6 97.8 %copy-start.15 = (bf16[512,12,64]{0,2,1:T(8,128)(2,1)S(1)}, bf16[512,12,64]{0,2,1:T(8,128)(2,1)}, u32[]{:S(2)}) copy-start(bf16[512,12,64]{0,2,1:T(8,128)(2,1)} %copy-done.14) | copy-start | bytes 2359300
  (31 other events, 49.8 us)
Sparse Core Ops, SparseCore 0:
  11.5 56.7 all-gather.10
  71.7 52.9 all-gather.8
  128.2 52.9 all-gather.12
  184.6 52.9 all-gather.14
  240.2 39.9 all-gather.18
  303.1 27.4 all-gather.16
  333.3 41.0 all-gather.20
  381.1 36.6 reduce-scatter.14
  425.6 28.5 all-gather.22
  470.6 37.9 reduce-scatter.16
  788.1 31.9 all-reduce.8
  823.7 64.1 reduce-scatter.22
  891.7 63.0 reduce-scatter.20
  959.3 70.2 all-reduce.6
  1036.2 98.1 reduce-scatter.18
  1140.1 98.0 reduce-scatter.24
  1244.7 98.0 reduce-scatter.26
  1348.5 98.1 reduce-scatter.28
